TPU v7x, 32 devices: a whole 2x2x4 slice. The times are simulated.
32 devices in a mesh: patch: 4 (over y, x), uly: 8 (over z, core).
Axes of the slice: x: 2, y: 2, z: 4, core: 2. Of those that a mesh axis runs over, the one named last changes fastest.
Arguments:
- queries: bfloat16 [512, 3072], P(('patch', 'uly')), may hold values from -512 to 512
- keys_new: bfloat16 [512, 3072], P(('patch', 'uly')), may hold values from -6 to 6
- values_new: bfloat16 [512, 3072], P(('patch', 'uly')), may hold values from -6 to 6
- keys_old: bfloat16 [512, 3072], P(('patch', 'uly')), may hold values from -8 to 8
- values_old: bfloat16 [512, 3072], P(('patch', 'uly')), may hold values from -6 to 6
- gate_table: float32 [50, 3072], replicated, may hold values from 0.5 to 2
- step_index: int32 [1], replicated, may hold values from 0 to 49
Outputs:
- attended: bfloat16 [512, 3072], P(('patch', 'uly'))
All inputs are finite; a program needn't handle non-finite values.
Results may differ from a plain program's by a relative error of at most 0.0045.
Values may be sent and summed in bfloat16 or wider, within the bound.
No kernel may reach another device: no remote copies, remote signals or barrier semaphores. Data moves between devices by JAX's collectives and lax.ppermute only.
A program may use at most 64 MiB of HBM per device.

v0:
```python
import functools

import jax
import jax.numpy as jnp
from jax import lax
from jax.experimental import pallas as pl
from jax.experimental.pallas import tpu as pltpu
from jax.sharding import PartitionSpec as P


HEADS = 24
HEAD_DIM = 128
MAX_DIRECT = 8


def absorb(carry, query_heads, key_piece, value_piece, masked):
    run_max, run_total, accumulated = carry
    score = jnp.einsum(
        "phd,khd->hpk", query_heads, key_piece, preferred_element_type=jnp.float32
    ) * HEAD_DIM ** (-0.5)
    score = jnp.where(masked[None, None, :], jnp.float32(-1e30), score)
    new_max = jnp.maximum(run_max, jnp.max(score, axis=-1))
    shrink = jnp.exp(run_max - new_max)
    expo = jnp.exp(score - new_max[..., None])
    run_total = run_total * shrink + jnp.sum(expo, axis=-1)
    update = jnp.einsum(
        "hpk,khd->phd", expo.astype(jnp.bfloat16), value_piece, preferred_element_type=jnp.float32
    )
    accumulated = accumulated * jnp.transpose(shrink)[..., None] + update
    return (new_max, run_total, accumulated)


def absorb_blocks(carry, query_heads, key_piece, value_piece, masked):
    count = key_piece.shape[0]
    span = 2048
    if count > span and count % span == 0:
        heads_here = key_piece.shape[1]
        key_blocks = key_piece.reshape(count // span, span, heads_here, HEAD_DIM)
        value_blocks = value_piece.reshape(count // span, span, heads_here, HEAD_DIM)
        mask_blocks = masked.reshape(count // span, span)

        def one_block(state, pieces):
            return (absorb(state, query_heads, pieces[0], pieces[1], pieces[2]), None)

        carry, _ = lax.scan(one_block, carry, (key_blocks, value_blocks, mask_blocks))
        return carry
    return absorb(carry, query_heads, key_piece, value_piece, masked)


def body_many(queries, keys_new, values_new, keys_old, values_old, gate_table, step_index):
    groups = lax.axis_size("uly")
    heads_here = HEADS // groups
    width_here = heads_here * HEAD_DIM
    patch_here = lax.axis_index("patch")
    fresh = (
        lax.all_to_all(queries, "uly", split_axis=1, concat_axis=0, tiled=True),
        lax.all_to_all(keys_new, "uly", split_axis=1, concat_axis=0, tiled=True),
        lax.all_to_all(values_new, "uly", split_axis=1, concat_axis=0, tiled=True),
    )
    query_heads = fresh[0].reshape(-1, heads_here, HEAD_DIM)
    fresh_keys = fresh[1].reshape(-1, heads_here, HEAD_DIM)
    fresh_values = fresh[2].reshape(-1, heads_here, HEAD_DIM)
    patch_rows = query_heads.shape[0]
    score = jnp.einsum(
        "phd,khd->hpk", query_heads, fresh_keys, preferred_element_type=jnp.float32
    ) * HEAD_DIM ** (-0.5)
    run_max = jnp.max(score, axis=-1)
    expo = jnp.exp(score - run_max[..., None])
    run_total = jnp.sum(expo, axis=-1)
    accumulated = jnp.einsum(
        "hpk,khd->phd", expo.astype(jnp.bfloat16), fresh_values, preferred_element_type=jnp.float32
    )
    carry = (run_max, run_total, accumulated)
    stale = (
        lax.all_to_all(keys_old, "uly", split_axis=1, concat_axis=0, tiled=True),
        lax.all_to_all(values_old, "uly", split_axis=1, concat_axis=0, tiled=True),
    )
    stale_keys = stale[0].reshape(-1, heads_here, HEAD_DIM)
    stale_values = stale[1].reshape(-1, heads_here, HEAD_DIM)
    pieces = (
        lax.all_gather(stale_keys, "patch", axis=0, tiled=True),
        lax.all_gather(stale_values, "patch", axis=0, tiled=True),
    )
    count = pieces[0].shape[0]
    masked = jnp.arange(count, dtype=jnp.int32) // patch_rows == patch_here
    carry = absorb_blocks(carry, query_heads, pieces[0], pieces[1], masked)
    run_max, run_total, accumulated = carry
    picker = (jnp.arange(gate_table.shape[0], dtype=jnp.int32) == step_index[0]).astype(jnp.float32)
    gate = jnp.dot(picker, gate_table, precision=lax.Precision.HIGHEST)
    gate_here = lax.dynamic_slice_in_dim(gate, lax.axis_index("uly") * width_here, width_here, 0)
    mixed = (accumulated / jnp.transpose(run_total)[..., None]).reshape(patch_rows, width_here)
    gated = (mixed * gate_here).astype(jnp.bfloat16)
    return lax.all_to_all(gated, "uly", split_axis=0, concat_axis=1, tiled=True)


def steps_of(count):
    return [0] + list(range(max(count // 2, 1), count)) + list(reversed(range(1, count // 2)))


def out_steps_of(count):
    return [0] + [step for step in (count - 1, *range(1, count - 1)) if step > 0]


def partner(here, step, count):
    if count & (count - 1) == 0:
        return here ^ step
    return (here + step) % count


def source(here, step, count):
    if count & (count - 1) == 0:
        return here ^ step
    return (here - step) % count


def shift(array, axis, step, lane, count, way=partner):
    pairs = [(i * lane + j, way(i, step, count) * lane + j) for i in range(count) for j in range(lane)]
    return lax.ppermute(array, axis, pairs)


def swap(array):
    return lax.ppermute(array, "uly", [(i, i ^ 1) for i in range(lax.axis_size("uly"))])


def in_vmem(array):
    return pltpu.with_memory_space_constraint(array, pltpu.VMEM)


def pack_kernel(steps, levels, width, level_ref, *refs):
    count = len(refs) - len(steps)
    level = level_ref[0]
    for step, out_ref in zip(steps, refs[count:], strict=True):
        column = pl.multiple_of(partner(level, step, levels) * width, HEAD_DIM)
        for place, ref in enumerate(refs[:count]):
            rows = ref.shape[0]
            out_ref[pl.ds(place * rows, rows), :] = ref[:, pl.ds(column, width)]


def pack(level, arrays, steps, levels, width):
    rows = arrays[0].shape[0] * len(arrays)
    vmem = pl.BlockSpec(memory_space=pltpu.VMEM)
    return pl.pallas_call(
        functools.partial(pack_kernel, steps, levels, width),
        out_shape=[pltpu.VMEM((rows, width), arrays[0].dtype)] * len(steps),
        in_specs=[pl.BlockSpec(memory_space=pltpu.SMEM)] + [vmem] * len(arrays),
        out_specs=[vmem] * len(steps),
    )(level, *arrays)


def attend_kernel(places, rows, heads_here, sides, others, gate_ref, *refs):
    levels = len(places)
    fresh = refs[: sides * levels]
    stale = refs[sides * levels : sides * (levels + others)]
    outs = refs[sides * (levels + others) :]
    nearest = (((1,), (1,)), ((), ()))
    plain = (((1,), (0,)), ((), ()))
    for head in range(heads_here):
        columns = slice(head * HEAD_DIM, (head + 1) * HEAD_DIM)
        query = jnp.concatenate([r[0:rows, columns] for r in fresh[:levels]], axis=0)
        keys = [r[rows : 2 * rows, columns] for r in fresh]
        values = [r[2 * rows : 3 * rows, columns] for r in fresh]
        for r in stale:
            keys += [r[i, 0:rows, columns] for i in range(levels)]
            values += [r[i, rows : 2 * rows, columns] for i in range(levels)]
        key = jnp.concatenate(keys, axis=0)
        value = jnp.concatenate(values, axis=0)
        score = lax.dot_general(
            query, key, nearest, preferred_element_type=jnp.float32
        ) * HEAD_DIM ** (-0.5)
        expo = jnp.exp(score - jnp.max(score, axis=-1, keepdims=True))
        total = jnp.sum(expo, axis=-1, keepdims=True)
        summed = lax.dot_general(
            expo.astype(jnp.bfloat16), value, plain, preferred_element_type=jnp.float32
        )
        gated = ((summed / total) * gate_ref[0:1, columns]).astype(jnp.bfloat16)
        for place, out_ref in zip(places, outs, strict=True):
            out_ref[:, columns] = gated[place * rows : (place + 1) * rows, :]


def join_kernel(steps, levels, width, level_ref, *refs):
    out_ref = refs[-1]
    level = level_ref[0]
    for step, ref in zip(steps, refs[:-1], strict=True):
        column = pl.multiple_of(source(level, step, levels) * width, HEAD_DIM)
        out_ref[:, pl.ds(column, width)] = ref[...]


def body_few(queries, keys_new, values_new, keys_old, values_old, gate_table, step_index):
    groups = lax.axis_size("uly")
    patches = lax.axis_size("patch")
    lane = 2
    levels = groups // lane
    heads_here = HEADS // levels
    width = heads_here * HEAD_DIM
    rows = queries.shape[0]
    level = lax.axis_index("uly").astype(jnp.int32) // lane
    index = level.reshape(1)
    stale_steps = steps = steps_of(levels)
    out_steps = out_steps_of(levels)
    places = [steps.index(step) for step in out_steps]
    vmem = pl.BlockSpec(memory_space=pltpu.VMEM)
    smem = pl.BlockSpec(memory_space=pltpu.SMEM)

    def exchange(pieces, order, way):
        result = [pieces[0]]
        for step, piece in zip(order[1:], pieces[1:], strict=True):
            result.append(shift(piece, "uly", step, lane, levels, way))
        return result

    def swap_all(pieces):
        result = []
        for piece in pieces:
            result.append(swap(piece))
        return result

    stale_out = pack(index, (keys_old, values_old), stale_steps, levels, width)
    stale_here = jnp.stack(exchange(stale_out, stale_steps, partner))
    fresh_out = pack(index, (queries, keys_new, values_new), steps, levels, width)
    gate_here = lax.dynamic_slice(gate_table, (step_index[0], level * width), (1, width))
    stale_here, fresh_out, gate_here = lax.optimization_barrier((stale_here, fresh_out, gate_here))
    stale = []
    for step in reversed(range(1, patches)):
        stale.append(shift(stale_here, "patch", step, 1, patches))
    fresh = exchange(fresh_out, steps, partner)
    stale += swap_all(stale)
    fresh += swap_all(fresh)

    attended = pl.pallas_call(
        functools.partial(attend_kernel, places, rows, heads_here, lane, patches - 1),
        out_shape=[pltpu.VMEM((rows, width), jnp.bfloat16)] * levels,
        in_specs=[vmem] * (1 + len(fresh) + len(stale)),
        out_specs=[vmem] * levels,
        name="attend",
    )(*[in_vmem(x) for x in (gate_here, *fresh, *stale)])
    pieces = exchange(attended, out_steps, source)
    return pl.pallas_call(
        functools.partial(join_kernel, out_steps, levels, width),
        out_shape=jax.ShapeDtypeStruct((rows, levels * width), jnp.bfloat16),
        in_specs=[smem] + [vmem] * levels,
        out_specs=vmem,
        name="join",
    )(index, *[in_vmem(x) for x in pieces])


def solution(mesh):
    direct = 1 < mesh.shape["patch"] <= MAX_DIRECT and mesh.shape["uly"] % 4 == 0
    body = body_few if direct else body_many
    in_specs = (
        P(("patch", "uly"), None),
        P(("patch", "uly"), None),
        P(("patch", "uly"), None),
        P(("patch", "uly"), None),
        P(("patch", "uly"), None),
        P(),
        P(),
    )
    out_specs = P(("patch", "uly"), None)

    return jax.shard_map(body, mesh=mesh, in_specs=in_specs, out_specs=out_specs, check_vma=False)
```

profile of v0, /device:TPU:0, one launch (start us, length us, event | category | flops | bytes accessed | tf_op | source)
XLA Modules:
  0.0 37.4 jit_solution(11853467462551467591)
XLA Ops:
  0.0 1.0 %shard_map.73 = (bf16[32,768]{1,0:T(8,128)(2,1)S(1)}, bf16[32,768]{1,0:T(8,128)(2,1)S(1)}, bf16[32,768]{1,0:T(8,128)(2,1)S(1)}, bf16[32,768]{1,0:T(8,128)(2,1)S(1)}) custom-call(s32[1]{0:T(128)} %bitcast.level_ref, bf16[16,3072]{1,0:T(8,128)(2,1)} %refs_0_.2, bf16[16,3072]{1,0:T(8,128)(2,1)} %refs_1_.2), custom_call_target="tpu_custom_call" | custom-call | tf_op jit(solution)/shard_map/pallas_call | solution.py:142
  1.0 4.1 %collective-permute-start = (bf16[32,768]{1,0:T(8,128)(2,1)S(1)}, bf16[32,768]{1,0:T(8,128)(2,1)S(1)}, u32[]{:S(2)}, u32[]{:S(2)}) collective-permute-start(bf16[32,768]{1,0:T(8,128)(2,1)S(1)} %get-tuple-element.24), channel_id=1, source_target_pairs={{0,4},{1,5},{2,6},{3,7},{4,0},{5,1},{6,2},{7,3},{8,12},{9,13},{10,... | collective-permute-start | bytes 147464 | tf_op jit(solution)/shard_map/ppermute | solution.py:118
  5.1 1.3 %collective-permute-start.1 = (bf16[32,768]{1,0:T(8,128)(2,1)S(1)}, bf16[32,768]{1,0:T(8,128)(2,1)S(1)}, u32[]{:S(2)}, u32[]{:S(2)}) collective-permute-start(bf16[32,768]{1,0:T(8,128)(2,1)S(1)} %get-tuple-element.25), channel_id=1, source_target_pairs={{0,6},{1,7},{2,4},{3,5},{4,2},{5,3},{6,0},{7,1},{8,14},{9,15},{10,... | collective-permute-start | bytes 147464 | tf_op jit(solution)/shard_map/ppermute | solution.py:118
  7.3 0.8 %dynamic_slice.3.gate_ref = f32[1,768]{1,0:T(1,128)S(1)} dynamic-slice(f32[50,3072]{1,0:T(8,128)} %param.12, s32[]{:T(128)S(6)} %select_n.12, s32[]{:T(128)S(6)} %select_n.13), dynamic_slice_sizes={1,768} | dynamic-slice | bytes 6148 | tf_op jit(solution)/shard_map/dynamic_slice | solution.py:219
  8.1 1.0 %shard_map.74 = (bf16[48,768]{1,0:T(8,128)(2,1)S(1)}, bf16[48,768]{1,0:T(8,128)(2,1)S(1)}, bf16[48,768]{1,0:T(8,128)(2,1)S(1)}, bf16[48,768]{1,0:T(8,128)(2,1)S(1)}) custom-call(s32[1]{0:T(128)} %bitcast.level_ref, bf16[16,3072]{1,0:T(8,128)(2,1)} %refs_0_.3, bf16[16,3072]{1,0:T(8,128)(2,1)} %refs_1_.3, bf16[16,3072]{1,0:T(8,128)(2,1)} %refs_2_.1), custom_call_target="tpu_custom_call" | custom-call | tf_op jit(solution)/shard_map/pallas_call | solution.py:142
  9.2 1.9 %collective-permute-done.1 = bf16[32,768]{1,0:T(8,128)(2,1)S(1)} collective-permute-done((bf16[32,768]{1,0:T(8,128)(2,1)S(1)}, bf16[32,768]{1,0:T(8,128)(2,1)S(1)}, u32[]{:S(2)}, u32[]{:S(2)}) %collective-permute-start.1) | collective-permute-done | bytes 49184 | tf_op jit(solution)/shard_map/ppermute | solution.py:118
  11.1 1.6 %collective-permute-start.12 = (bf16[4,32,768]{2,1,0:T(8,128)(2,1)S(1)}, bf16[4,32,768]{2,1,0:T(8,128)(2,1)S(1)}, u32[]{:S(2)}, u32[]{:S(2)}) collective-permute-start(bf16[4,32,768]{2,1,0:T(8,128)(2,1)S(1)} %pad_maximum_fusion), channel_id=1, source_target_pairs={{0,8},{8,0},{16,24},{24,16},{1,9},{9,1},{17,25},{25,17},{2,10},{10... | collective-permute-start | bytes 589832 | tf_op jit(solution)/shard_map/ppermute | solution.py:118
  12.6 1.5 %collective-permute-start.11 = (bf16[4,32,768]{2,1,0:T(8,128)(2,1)S(1)}, bf16[4,32,768]{2,1,0:T(8,128)(2,1)S(1)}, u32[]{:S(2)}, u32[]{:S(2)}) collective-permute-start(bf16[4,32,768]{2,1,0:T(8,128)(2,1)S(1)} %pad_maximum_fusion), channel_id=1, source_target_pairs={{0,16},{8,24},{16,0},{24,8},{1,17},{9,25},{17,1},{25,9},{2,18},{10... | collective-permute-start | bytes 589832 | tf_op jit(solution)/shard_map/ppermute | solution.py:118
  14.6 1.6 %collective-permute-start.3 = (bf16[48,768]{1,0:T(8,128)(2,1)S(1)}, bf16[48,768]{1,0:T(8,128)(2,1)S(1)}, u32[]{:S(2)}, u32[]{:S(2)}) collective-permute-start(bf16[48,768]{1,0:T(8,128)(2,1)S(1)} %get-tuple-element.33), channel_id=1, source_target_pairs={{0,4},{1,5},{2,6},{3,7},{4,0},{5,1},{6,2},{7,3},{8,12},{9,13},{10,... | collective-permute-start | bytes 221192 | tf_op jit(solution)/shard_map/ppermute | solution.py:118
  16.2 1.0 %collective-permute-start.4 = (bf16[48,768]{1,0:T(8,128)(2,1)S(1)}, bf16[48,768]{1,0:T(8,128)(2,1)S(1)}, u32[]{:S(2)}, u32[]{:S(2)}) collective-permute-start(bf16[48,768]{1,0:T(8,128)(2,1)S(1)} %get-tuple-element.34), channel_id=1, source_target_pairs={{0,6},{1,7},{2,4},{3,5},{4,2},{5,3},{6,0},{7,1},{8,14},{9,15},{10,... | collective-permute-start | bytes 221192 | tf_op jit(solution)/shard_map/ppermute | solution.py:118
  17.2 3.9 %collective-permute-done.3.refs_1_ = bf16[48,768]{1,0:T(8,128)(2,1)S(1)} collective-permute-done((bf16[48,768]{1,0:T(8,128)(2,1)S(1)}, bf16[48,768]{1,0:T(8,128)(2,1)S(1)}, u32[]{:S(2)}, u32[]{:S(2)}) %collective-permute-start.3) | collective-permute-done | bytes 73760 | tf_op jit(solution)/shard_map/ppermute | solution.py:118
  21.2 0.9 %collective-permute-done.11.refs_9_ = bf16[4,32,768]{2,1,0:T(8,128)(2,1)S(1)} collective-permute-done((bf16[4,32,768]{2,1,0:T(8,128)(2,1)S(1)}, bf16[4,32,768]{2,1,0:T(8,128)(2,1)S(1)}, u32[]{:S(2)}, u32[]{:S(2)}) %collective-permute-start.11) | collective-permute-done | bytes 196640 | tf_op jit(solution)/shard_map/ppermute | solution.py:118
  22.0 0.5 %collective-permute-start.13 = (bf16[4,32,768]{2,1,0:T(8,128)(2,1)S(1)}, bf16[4,32,768]{2,1,0:T(8,128)(2,1)S(1)}, u32[]{:S(2)}, u32[]{:S(2)}) collective-permute-start(bf16[4,32,768]{2,1,0:T(8,128)(2,1)S(1)} %collective-permute-done.10.refs_8_), channel_id=1, source_target_pairs={{0,1},{1,0},{2,3},{3,2},{4,5},{5,4},{6,7},{7,6},{8,9},{9,8},{10,11... | collective-permute-start | bytes 589832 | tf_op jit(solution)/shard_map/ppermute | solution.py:122
  22.7 2.8 %collective-permute-done.5.refs_3_ = bf16[48,768]{1,0:T(8,128)(2,1)S(1)} collective-permute-done((bf16[48,768]{1,0:T(8,128)(2,1)S(1)}, bf16[48,768]{1,0:T(8,128)(2,1)S(1)}, u32[]{:S(2)}, u32[]{:S(2)}) %collective-permute-start.5) | collective-permute-done | bytes 73760 | tf_op jit(solution)/shard_map/ppermute | solution.py:118
  25.5 0.5 %collective-permute-start.8 = (bf16[48,768]{1,0:T(8,128)(2,1)S(1)}, bf16[48,768]{1,0:T(8,128)(2,1)S(1)}, u32[]{:S(2)}, u32[]{:S(2)}) collective-permute-start(bf16[48,768]{1,0:T(8,128)(2,1)S(1)} %collective-permute-done.4.refs_2_), channel_id=1, source_target_pairs={{0,1},{1,0},{2,3},{3,2},{4,5},{5,4},{6,7},{7,6},{8,9},{9,8},{10,11... | collective-permute-start | bytes 221192 | tf_op jit(solution)/shard_map/ppermute | solution.py:122
  26.0 0.8 %collective-permute-done.7.refs_5_ = bf16[48,768]{1,0:T(8,128)(2,1)S(1)} collective-permute-done((bf16[48,768]{1,0:T(8,128)(2,1)S(1)}, bf16[48,768]{1,0:T(8,128)(2,1)S(1)}, u32[]{:S(2)}, u32[]{:S(2)}) %collective-permute-start.7) | collective-permute-done | bytes 73760 | tf_op jit(solution)/shard_map/ppermute | solution.py:122
  26.9 1.1 %collective-permute-done.9.refs_7_ = bf16[48,768]{1,0:T(8,128)(2,1)S(1)} collective-permute-done((bf16[48,768]{1,0:T(8,128)(2,1)S(1)}, bf16[48,768]{1,0:T(8,128)(2,1)S(1)}, u32[]{:S(2)}, u32[]{:S(2)}) %collective-permute-start.9) | collective-permute-done | bytes 73760 | tf_op jit(solution)/shard_map/ppermute | solution.py:122
  28.0 1.7 %attend.1 = (bf16[16,768]{1,0:T(8,128)(2,1)S(1)}, bf16[16,768]{1,0:T(8,128)(2,1)S(1)}, bf16[16,768]{1,0:T(8,128)(2,1)S(1)}, bf16[16,768]{1,0:T(8,128)(2,1)S(1)}) custom-call(f32[1,768]{1,0:T(1,128)S(1)} %dynamic_slice.3.gate_ref, bf16[48,768]{1,0:T(8,128)(2,1)S(1)} %get-tuple-element.32.refs_0_, bf16[48,768]{1,0:T(8,128)(2,1)S(1)} %collective-permute-done.3.refs_1_, ...), custom_call_target="tpu_custom_call" | custom-call | tf_op jit(solution)/shard_map/attend/pallas_call | solution.py:228
  29.7 2.1 %collective-permute-start.16 = (bf16[16,768]{1,0:T(8,128)(2,1)S(1)}, bf16[16,768]{1,0:T(8,128)(2,1)S(1)}, u32[]{:S(2)}, u32[]{:S(2)}) collective-permute-start(bf16[16,768]{1,0:T(8,128)(2,1)S(1)} %get-tuple-element.38), channel_id=1, source_target_pairs={{0,6},{1,7},{2,4},{3,5},{4,2},{5,3},{6,0},{7,1},{8,14},{9,15},{10,... | collective-permute-start | bytes 73736 | tf_op jit(solution)/shard_map/ppermute | solution.py:118
  31.8 2.3 %collective-permute-start.18 = (bf16[16,768]{1,0:T(8,128)(2,1)S(1)}, bf16[16,768]{1,0:T(8,128)(2,1)S(1)}, u32[]{:S(2)}, u32[]{:S(2)}) collective-permute-start(bf16[16,768]{1,0:T(8,128)(2,1)S(1)} %get-tuple-element.40), channel_id=1, source_target_pairs={{0,4},{1,5},{2,6},{3,7},{4,0},{5,1},{6,2},{7,3},{8,12},{9,13},{10,... | collective-permute-start | bytes 73736 | tf_op jit(solution)/shard_map/ppermute | solution.py:118
  34.1 1.3 %collective-permute-done.16.refs_1_ = bf16[16,768]{1,0:T(8,128)(2,1)S(1)} collective-permute-done((bf16[16,768]{1,0:T(8,128)(2,1)S(1)}, bf16[16,768]{1,0:T(8,128)(2,1)S(1)}, u32[]{:S(2)}, u32[]{:S(2)}) %collective-permute-start.16) | collective-permute-done | bytes 24608 | tf_op jit(solution)/shard_map/ppermute | solution.py:118
  35.4 0.5 %collective-permute-done.17.refs_2_ = bf16[16,768]{1,0:T(8,128)(2,1)S(1)} collective-permute-done((bf16[16,768]{1,0:T(8,128)(2,1)S(1)}, bf16[16,768]{1,0:T(8,128)(2,1)S(1)}, u32[]{:S(2)}, u32[]{:S(2)}) %collective-permute-start.17) | collective-permute-done | bytes 24608 | tf_op jit(solution)/shard_map/ppermute | solution.py:118
  35.9 0.9 %collective-permute-done.18.refs_3_ = bf16[16,768]{1,0:T(8,128)(2,1)S(1)} collective-permute-done((bf16[16,768]{1,0:T(8,128)(2,1)S(1)}, bf16[16,768]{1,0:T(8,128)(2,1)S(1)}, u32[]{:S(2)}, u32[]{:S(2)}) %collective-permute-start.18) | collective-permute-done | bytes 24608 | tf_op jit(solution)/shard_map/ppermute | solution.py:118
  36.8 0.7 %join.1 = bf16[16,3072]{1,0:T(8,128)(2,1)} custom-call(s32[1]{0:T(128)} %bitcast.level_ref, bf16[16,768]{1,0:T(8,128)(2,1)S(1)} %get-tuple-element.37.refs_0_, bf16[16,768]{1,0:T(8,128)(2,1)S(1)} %collective-permute-done.16.refs_1_, bf16[16,768]{1,0:T(8,128)(2,1)S(1)} %collective-permute-done.17.refs_2_, bf16[16,768]{1,0:T(8,128)(2,1)S(1)} %collective-permute-done.18.refs_3_), custom_call_target="tpu_custom_call" | custom-call | tf_op jit(solution)/shard_map/join/pallas_call | solution.py:236
  (20 shorter events, 1.1 us)
Async XLA Ops:
  1.0 8.2 %collective-permute-start = (bf16[32,768]{1,0:T(8,128)(2,1)S(1)}, bf16[32,768]{1,0:T(8,128)(2,1)S(1)}, u32[]{:S(2)}, u32[]{:S(2)}) collective-permute-start(bf16[32,768]{1,0:T(8,128)(2,1)S(1)} %get-tuple-element.24), channel_id=1, source_target_pairs={{0,4},{1,5},{2,6},{3,7},{4,0},{5,1},{6,2},{7,3},{8,12},{9,13},{10,... | collective-permute-start | bytes 147464 | tf_op jit(solution)/shard_map/ppermute | solution.py:118
  5.1 6.0 %collective-permute-start.1 = (bf16[32,768]{1,0:T(8,128)(2,1)S(1)}, bf16[32,768]{1,0:T(8,128)(2,1)S(1)}, u32[]{:S(2)}, u32[]{:S(2)}) collective-permute-start(bf16[32,768]{1,0:T(8,128)(2,1)S(1)} %get-tuple-element.25), channel_id=1, source_target_pairs={{0,6},{1,7},{2,4},{3,5},{4,2},{5,3},{6,0},{7,1},{8,14},{9,15},{10,... | collective-permute-start | bytes 147464 | tf_op jit(solution)/shard_map/ppermute | solution.py:118
  6.4 4.6 %collective-permute-start.2 = (bf16[32,768]{1,0:T(8,128)(2,1)S(1)}, bf16[32,768]{1,0:T(8,128)(2,1)S(1)}, u32[]{:S(2)}, u32[]{:S(2)}) collective-permute-start(bf16[32,768]{1,0:T(8,128)(2,1)S(1)} %get-tuple-element.26), channel_id=1, source_target_pairs={{0,2},{1,3},{2,0},{3,1},{4,6},{5,7},{6,4},{7,5},{8,10},{9,11},{10,... | collective-permute-start | bytes 147464 | tf_op jit(solution)/shard_map/ppermute | solution.py:118
  11.1 10.1 %collective-permute-start.12 = (bf16[4,32,768]{2,1,0:T(8,128)(2,1)S(1)}, bf16[4,32,768]{2,1,0:T(8,128)(2,1)S(1)}, u32[]{:S(2)}, u32[]{:S(2)}) collective-permute-start(bf16[4,32,768]{2,1,0:T(8,128)(2,1)S(1)} %pad_maximum_fusion), channel_id=1, source_target_pairs={{0,8},{8,0},{16,24},{24,16},{1,9},{9,1},{17,25},{25,17},{2,10},{10... | collective-permute-start | bytes 589832 | tf_op jit(solution)/shard_map/ppermute | solution.py:118
  12.6 9.4 %collective-permute-start.11 = (bf16[4,32,768]{2,1,0:T(8,128)(2,1)S(1)}, bf16[4,32,768]{2,1,0:T(8,128)(2,1)S(1)}, u32[]{:S(2)}, u32[]{:S(2)}) collective-permute-start(bf16[4,32,768]{2,1,0:T(8,128)(2,1)S(1)} %pad_maximum_fusion), channel_id=1, source_target_pairs={{0,16},{8,24},{16,0},{24,8},{1,17},{9,25},{17,1},{25,9},{2,18},{10... | collective-permute-start | bytes 589832 | tf_op jit(solution)/shard_map/ppermute | solution.py:118
  14.2 7.9 %collective-permute-start.10 = (bf16[4,32,768]{2,1,0:T(8,128)(2,1)S(1)}, bf16[4,32,768]{2,1,0:T(8,128)(2,1)S(1)}, u32[]{:S(2)}, u32[]{:S(2)}) collective-permute-start(bf16[4,32,768]{2,1,0:T(8,128)(2,1)S(1)} %pad_maximum_fusion), channel_id=1, source_target_pairs={{0,24},{8,16},{16,8},{24,0},{1,25},{9,17},{17,9},{25,1},{2,26},{10... | collective-permute-start | bytes 589832 | tf_op jit(solution)/shard_map/ppermute | solution.py:118
  14.6 6.5 %collective-permute-start.3 = (bf16[48,768]{1,0:T(8,128)(2,1)S(1)}, bf16[48,768]{1,0:T(8,128)(2,1)S(1)}, u32[]{:S(2)}, u32[]{:S(2)}) collective-permute-start(bf16[48,768]{1,0:T(8,128)(2,1)S(1)} %get-tuple-element.33), channel_id=1, source_target_pairs={{0,4},{1,5},{2,6},{3,7},{4,0},{5,1},{6,2},{7,3},{8,12},{9,13},{10,... | collective-permute-start | bytes 221192 | tf_op jit(solution)/shard_map/ppermute | solution.py:118
  16.2 6.5 %collective-permute-start.4 = (bf16[48,768]{1,0:T(8,128)(2,1)S(1)}, bf16[48,768]{1,0:T(8,128)(2,1)S(1)}, u32[]{:S(2)}, u32[]{:S(2)}) collective-permute-start(bf16[48,768]{1,0:T(8,128)(2,1)S(1)} %get-tuple-element.34), channel_id=1, source_target_pairs={{0,6},{1,7},{2,4},{3,5},{4,2},{5,3},{6,0},{7,1},{8,14},{9,15},{10,... | collective-permute-start | bytes 221192 | tf_op jit(solution)/shard_map/ppermute | solution.py:118
  21.1 4.4 %collective-permute-start.5 = (bf16[48,768]{1,0:T(8,128)(2,1)S(1)}, bf16[48,768]{1,0:T(8,128)(2,1)S(1)}, u32[]{:S(2)}, u32[]{:S(2)}) collective-permute-start(bf16[48,768]{1,0:T(8,128)(2,1)S(1)} %get-tuple-element.35), channel_id=1, source_target_pairs={{0,2},{1,3},{2,0},{3,1},{4,6},{5,7},{6,4},{7,5},{8,10},{9,11},{10,... | collective-permute-start | bytes 221192 | tf_op jit(solution)/shard_map/ppermute | solution.py:118
  21.1 6.9 %collective-permute-start.15 = (bf16[4,32,768]{2,1,0:T(8,128)(2,1)S(1)}, bf16[4,32,768]{2,1,0:T(8,128)(2,1)S(1)}, u32[]{:S(2)}, u32[]{:S(2)}) collective-permute-start(bf16[4,32,768]{2,1,0:T(8,128)(2,1)S(1)} %collective-permute-done.12.refs_10_), channel_id=1, source_target_pairs={{0,1},{1,0},{2,3},{3,2},{4,5},{5,4},{6,7},{7,6},{8,9},{9,8},{10,11... | collective-permute-start | bytes 589832 | tf_op jit(solution)/shard_map/ppermute | solution.py:122
  22.0 6.0 %collective-permute-start.14 = (bf16[4,32,768]{2,1,0:T(8,128)(2,1)S(1)}, bf16[4,32,768]{2,1,0:T(8,128)(2,1)S(1)}, u32[]{:S(2)}, u32[]{:S(2)}) collective-permute-start(bf16[4,32,768]{2,1,0:T(8,128)(2,1)S(1)} %collective-permute-done.11.refs_9_), channel_id=1, source_target_pairs={{0,1},{1,0},{2,3},{3,2},{4,5},{5,4},{6,7},{7,6},{8,9},{9,8},{10,11... | collective-permute-start | bytes 589832 | tf_op jit(solution)/shard_map/ppermute | solution.py:122
  22.0 6.0 %collective-permute-start.13 = (bf16[4,32,768]{2,1,0:T(8,128)(2,1)S(1)}, bf16[4,32,768]{2,1,0:T(8,128)(2,1)S(1)}, u32[]{:S(2)}, u32[]{:S(2)}) collective-permute-start(bf16[4,32,768]{2,1,0:T(8,128)(2,1)S(1)} %collective-permute-done.10.refs_8_), channel_id=1, source_target_pairs={{0,1},{1,0},{2,3},{3,2},{4,5},{5,4},{6,7},{7,6},{8,9},{9,8},{10,11... | collective-permute-start | bytes 589832 | tf_op jit(solution)/shard_map/ppermute | solution.py:122
  22.7 2.8 %collective-permute-start.6 = (bf16[48,768]{1,0:T(8,128)(2,1)S(1)}, bf16[48,768]{1,0:T(8,128)(2,1)S(1)}, u32[]{:S(2)}, u32[]{:S(2)}) collective-permute-start(bf16[48,768]{1,0:T(8,128)(2,1)S(1)} %get-tuple-element.32.refs_0_), channel_id=1, source_target_pairs={{0,1},{1,0},{2,3},{3,2},{4,5},{5,4},{6,7},{7,6},{8,9},{9,8},{10,11... | collective-permute-start | bytes 221192 | tf_op jit(solution)/shard_map/ppermute | solution.py:122
  25.5 1.3 %collective-permute-start.7 = (bf16[48,768]{1,0:T(8,128)(2,1)S(1)}, bf16[48,768]{1,0:T(8,128)(2,1)S(1)}, u32[]{:S(2)}, u32[]{:S(2)}) collective-permute-start(bf16[48,768]{1,0:T(8,128)(2,1)S(1)} %collective-permute-done.3.refs_1_), channel_id=1, source_target_pairs={{0,1},{1,0},{2,3},{3,2},{4,5},{5,4},{6,7},{7,6},{8,9},{9,8},{10,11... | collective-permute-start | bytes 221192 | tf_op jit(solution)/shard_map/ppermute | solution.py:122
  25.5 1.4 %collective-permute-start.8 = (bf16[48,768]{1,0:T(8,128)(2,1)S(1)}, bf16[48,768]{1,0:T(8,128)(2,1)S(1)}, u32[]{:S(2)}, u32[]{:S(2)}) collective-permute-start(bf16[48,768]{1,0:T(8,128)(2,1)S(1)} %collective-permute-done.4.refs_2_), channel_id=1, source_target_pairs={{0,1},{1,0},{2,3},{3,2},{4,5},{5,4},{6,7},{7,6},{8,9},{9,8},{10,11... | collective-permute-start | bytes 221192 | tf_op jit(solution)/shard_map/ppermute | solution.py:122
  26.8 1.3 %collective-permute-start.9 = (bf16[48,768]{1,0:T(8,128)(2,1)S(1)}, bf16[48,768]{1,0:T(8,128)(2,1)S(1)}, u32[]{:S(2)}, u32[]{:S(2)}) collective-permute-start(bf16[48,768]{1,0:T(8,128)(2,1)S(1)} %collective-permute-done.5.refs_3_), channel_id=1, source_target_pairs={{0,1},{1,0},{2,3},{3,2},{4,5},{5,4},{6,7},{7,6},{8,9},{9,8},{10,11... | collective-permute-start | bytes 221192 | tf_op jit(solution)/shard_map/ppermute | solution.py:122
  29.7 5.7 %collective-permute-start.16 = (bf16[16,768]{1,0:T(8,128)(2,1)S(1)}, bf16[16,768]{1,0:T(8,128)(2,1)S(1)}, u32[]{:S(2)}, u32[]{:S(2)}) collective-permute-start(bf16[16,768]{1,0:T(8,128)(2,1)S(1)} %get-tuple-element.38), channel_id=1, source_target_pairs={{0,6},{1,7},{2,4},{3,5},{4,2},{5,3},{6,0},{7,1},{8,14},{9,15},{10,... | collective-permute-start | bytes 73736 | tf_op jit(solution)/shard_map/ppermute | solution.py:118
  31.8 4.1 %collective-permute-start.17 = (bf16[16,768]{1,0:T(8,128)(2,1)S(1)}, bf16[16,768]{1,0:T(8,128)(2,1)S(1)}, u32[]{:S(2)}, u32[]{:S(2)}) collective-permute-start(bf16[16,768]{1,0:T(8,128)(2,1)S(1)} %get-tuple-element.39), channel_id=1, source_target_pairs={{0,2},{1,3},{2,0},{3,1},{4,6},{5,7},{6,4},{7,5},{8,10},{9,11},{10,... | collective-permute-start | bytes 73736 | tf_op jit(solution)/shard_map/ppermute | solution.py:118
  31.8 5.0 %collective-permute-start.18 = (bf16[16,768]{1,0:T(8,128)(2,1)S(1)}, bf16[16,768]{1,0:T(8,128)(2,1)S(1)}, u32[]{:S(2)}, u32[]{:S(2)}) collective-permute-start(bf16[16,768]{1,0:T(8,128)(2,1)S(1)} %get-tuple-element.40), channel_id=1, source_target_pairs={{0,4},{1,5},{2,6},{3,7},{4,0},{5,1},{6,2},{7,3},{8,12},{9,13},{10,... | collective-permute-start | bytes 73736 | tf_op jit(solution)/shard_map/ppermute | solution.py:118
where the time goes:
time: 37.7 us; the launch traced here: 37.4 us
  starting transfers between devices  17.5 us (46%)
  waiting for transfers between devices  14.1 us (37%)
  Pallas kernels  4.27 us (11%)
  local copies, waits for them, and re-layouts  0.82 us (2%)
  between operations  0.71 us (2%)
    ppermute x12, starting transfers between devices, shift(): return lax.ppermute(array, axis, pairs)  16.3 us
    ppermute x12, waiting for transfers between devices, shift(): return lax.ppermute(array, axis, pairs)  12.3 us
    pallas_call x2, Pallas kernels, pack(): pl.pallas_call(functools.partial(pack_kernel, steps, levels, width), out_...  1.97 us
    ppermute x7, waiting for transfers between devices, swap(): lax.ppermute(array, 'uly', [(i, i ^ 1) for i in range(lax.axis_size('uly'...  1.87 us
    pallas_call x1, Pallas kernels, body_few(): pl.pallas_call(functools.partial(attend_kernel, places, rows, heads_here,...  1.66 us
    ppermute x7, starting transfers between devices, swap(): lax.ppermute(array, 'uly', [(i, i ^ 1) for i in range(lax.axis_size('uly'...  1.18 us
    dynamic_slice x1, local copies, waits for them, and re-layouts, body_few(): lax.dynamic_slice(gate_table, (step_index[0], level * width), (1, width))  0.82 us
  transfers between devices with their start and end apart: 19, of which 10 were waited for; matrix products, arithmetic and copies ran while one was open for 2% of the time, Pallas kernels for 3%

commit v1 on v0

--- a/solution.py
+++ b/solution.py
@@ -98,7 +98,7 @@
 
 
 def out_steps_of(count):
-    return [0] + [step for step in (count - 1, *range(1, count - 1)) if step > 0]
+    return [0] + list(reversed(range(1, count)))
 
 
 def partner(here, step, count):
@@ -154,27 +154,36 @@
     outs = refs[sides * (levels + others) :]
     nearest = (((1,), (1,)), ((), ()))
     plain = (((1,), (0,)), ((), ()))
-    for head in range(heads_here):
+
+    def scores(head):
         columns = slice(head * HEAD_DIM, (head + 1) * HEAD_DIM)
         query = jnp.concatenate([r[0:rows, columns] for r in fresh[:levels]], axis=0)
         keys = [r[rows : 2 * rows, columns] for r in fresh]
+        for r in stale:
+            keys += [r[i, 0:rows, columns] for i in range(levels)]
+        key = jnp.concatenate(keys, axis=0)
+        return lax.dot_general(query, key, nearest, preferred_element_type=jnp.float32)
+
+    def weights(raw):
+        score = raw * HEAD_DIM ** (-0.5)
+        expo = jnp.exp(score - jnp.max(score, axis=-1, keepdims=True))
+        return expo.astype(jnp.bfloat16), jnp.sum(expo, axis=-1, keepdims=True)
+
+    def finish(head, weight, total):
+        columns = slice(head * HEAD_DIM, (head + 1) * HEAD_DIM)
         values = [r[2 * rows : 3 * rows, columns] for r in fresh]
         for r in stale:
-            keys += [r[i, 0:rows, columns] for i in range(levels)]
             values += [r[i, rows : 2 * rows, columns] for i in range(levels)]
-        key = jnp.concatenate(keys, axis=0)
         value = jnp.concatenate(values, axis=0)
-        score = lax.dot_general(
-            query, key, nearest, preferred_element_type=jnp.float32
-        ) * HEAD_DIM ** (-0.5)
-        expo = jnp.exp(score - jnp.max(score, axis=-1, keepdims=True))
-        total = jnp.sum(expo, axis=-1, keepdims=True)
-        summed = lax.dot_general(
-            expo.astype(jnp.bfloat16), value, plain, preferred_element_type=jnp.float32
-        )
+        summed = lax.dot_general(weight, value, plain, preferred_element_type=jnp.float32)
         gated = ((summed / total) * gate_ref[0:1, columns]).astype(jnp.bfloat16)
         for place, out_ref in zip(places, outs, strict=True):
             out_ref[:, columns] = gated[place * rows : (place + 1) * rows, :]
+
+    raw = [scores(head) for head in range(heads_here)]
+    soft = [weights(one) for one in raw]
+    for head, (weight, total) in enumerate(soft):
+        finish(head, weight, total)
 
 
 def join_kernel(steps, levels, width, level_ref, *refs):

time: 37.7 us -> 36.5 us (0.968)
  Pallas kernels: 4.27 us -> 3.3 us
    pallas_call x1, Pallas kernels: 1.66 us -> 0.69 us  [body_few(): pl.pallas_call(functools.partial(attend_kernel, places, rows, heads_here,...]
  transfers between devices with their start and end apart: 19 -> 19, of which waited for: 10 -> 9; matrix products, arithmetic and copies ran while one was open for 2% -> 2% of each run, Pallas kernels for 3% -> 3%
where the time goes in v1:
time: 36.5 us; the launch traced here: 36.2 us
  starting transfers between devices  17.5 us (48%)
  waiting for transfers between devices  13.9 us (38%)
  Pallas kernels  3.3 us (9%)
  local copies, waits for them, and re-layouts  0.82 us (2%)
  between operations  0.71 us (2%)
    ppermute x12, starting transfers between devices, shift(): return lax.ppermute(array, axis, pairs)  16.3 us
    ppermute x12, waiting for transfers between devices, shift(): return lax.ppermute(array, axis, pairs)  12 us
    pallas_call x2, Pallas kernels, pack(): pl.pallas_call(functools.partial(pack_kernel, steps, levels, width), out_...  1.97 us
    ppermute x7, waiting for transfers between devices, swap(): lax.ppermute(array, 'uly', [(i, i ^ 1) for i in range(lax.axis_size('uly'...  1.87 us
    ppermute x7, starting transfers between devices, swap(): lax.ppermute(array, 'uly', [(i, i ^ 1) for i in range(lax.axis_size('uly'...  1.18 us
    dynamic_slice x1, local copies, waits for them, and re-layouts, body_few(): lax.dynamic_slice(gate_table, (step_index[0], level * width), (1, width))  0.82 us
  transfers between devices with their start and end apart: 19, of which 9 were waited for; matrix products, arithmetic and copies ran while one was open for 2% of the time, Pallas kernels for 3%

profile of v1, /device:TPU:0, one launch (start us, length us, event | category | flops | bytes accessed | tf_op | source)
XLA Modules:
  0.0 36.2 jit_solution(12552173441352524952)
XLA Ops:
  0.0 1.0 %shard_map.73 = (bf16[32,768]{1,0:T(8,128)(2,1)S(1)}, bf16[32,768]{1,0:T(8,128)(2,1)S(1)}, bf16[32,768]{1,0:T(8,128)(2,1)S(1)}, bf16[32,768]{1,0:T(8,128)(2,1)S(1)}) custom-call(s32[1]{0:T(128)} %bitcast.level_ref, bf16[16,3072]{1,0:T(8,128)(2,1)} %refs_0_.2, bf16[16,3072]{1,0:T(8,128)(2,1)} %refs_1_.2), custom_call_target="tpu_custom_call" | custom-call | tf_op jit(solution)/shard_map/pallas_call | solution.py:142
  1.0 4.1 %collective-permute-start = (bf16[32,768]{1,0:T(8,128)(2,1)S(1)}, bf16[32,768]{1,0:T(8,128)(2,1)S(1)}, u32[]{:S(2)}, u32[]{:S(2)}) collective-permute-start(bf16[32,768]{1,0:T(8,128)(2,1)S(1)} %get-tuple-element.24), channel_id=1, source_target_pairs={{0,4},{1,5},{2,6},{3,7},{4,0},{5,1},{6,2},{7,3},{8,12},{9,13},{10,... | collective-permute-start | bytes 147464 | tf_op jit(solution)/shard_map/ppermute | solution.py:118
  5.1 1.3 %collective-permute-start.1 = (bf16[32,768]{1,0:T(8,128)(2,1)S(1)}, bf16[32,768]{1,0:T(8,128)(2,1)S(1)}, u32[]{:S(2)}, u32[]{:S(2)}) collective-permute-start(bf16[32,768]{1,0:T(8,128)(2,1)S(1)} %get-tuple-element.25), channel_id=1, source_target_pairs={{0,6},{1,7},{2,4},{3,5},{4,2},{5,3},{6,0},{7,1},{8,14},{9,15},{10,... | collective-permute-start | bytes 147464 | tf_op jit(solution)/shard_map/ppermute | solution.py:118
  7.3 0.8 %dynamic_slice.3.gate_ref = f32[1,768]{1,0:T(1,128)S(1)} dynamic-slice(f32[50,3072]{1,0:T(8,128)} %param.12, s32[]{:T(128)S(6)} %select_n.12, s32[]{:T(128)S(6)} %select_n.13), dynamic_slice_sizes={1,768} | dynamic-slice | bytes 6148 | tf_op jit(solution)/shard_map/dynamic_slice | solution.py:228
  8.1 1.0 %shard_map.74 = (bf16[48,768]{1,0:T(8,128)(2,1)S(1)}, bf16[48,768]{1,0:T(8,128)(2,1)S(1)}, bf16[48,768]{1,0:T(8,128)(2,1)S(1)}, bf16[48,768]{1,0:T(8,128)(2,1)S(1)}) custom-call(s32[1]{0:T(128)} %bitcast.level_ref, bf16[16,3072]{1,0:T(8,128)(2,1)} %refs_0_.3, bf16[16,3072]{1,0:T(8,128)(2,1)} %refs_1_.3, bf16[16,3072]{1,0:T(8,128)(2,1)} %refs_2_.1), custom_call_target="tpu_custom_call" | custom-call | tf_op jit(solution)/shard_map/pallas_call | solution.py:142
  9.2 1.9 %collective-permute-done.1 = bf16[32,768]{1,0:T(8,128)(2,1)S(1)} collective-permute-done((bf16[32,768]{1,0:T(8,128)(2,1)S(1)}, bf16[32,768]{1,0:T(8,128)(2,1)S(1)}, u32[]{:S(2)}, u32[]{:S(2)}) %collective-permute-start.1) | collective-permute-done | bytes 49184 | tf_op jit(solution)/shard_map/ppermute | solution.py:118
  11.1 1.6 %collective-permute-start.12 = (bf16[4,32,768]{2,1,0:T(8,128)(2,1)S(1)}, bf16[4,32,768]{2,1,0:T(8,128)(2,1)S(1)}, u32[]{:S(2)}, u32[]{:S(2)}) collective-permute-start(bf16[4,32,768]{2,1,0:T(8,128)(2,1)S(1)} %pad_maximum_fusion), channel_id=1, source_target_pairs={{0,8},{8,0},{16,24},{24,16},{1,9},{9,1},{17,25},{25,17},{2,10},{10... | collective-permute-start | bytes 589832 | tf_op jit(solution)/shard_map/ppermute | solution.py:118
  12.6 1.5 %collective-permute-start.11 = (bf16[4,32,768]{2,1,0:T(8,128)(2,1)S(1)}, bf16[4,32,768]{2,1,0:T(8,128)(2,1)S(1)}, u32[]{:S(2)}, u32[]{:S(2)}) collective-permute-start(bf16[4,32,768]{2,1,0:T(8,128)(2,1)S(1)} %pad_maximum_fusion), channel_id=1, source_target_pairs={{0,16},{8,24},{16,0},{24,8},{1,17},{9,25},{17,1},{25,9},{2,18},{10... | collective-permute-start | bytes 589832 | tf_op jit(solution)/shard_map/ppermute | solution.py:118
  14.2 0.5 %collective-permute-start.10 = (bf16[4,32,768]{2,1,0:T(8,128)(2,1)S(1)}, bf16[4,32,768]{2,1,0:T(8,128)(2,1)S(1)}, u32[]{:S(2)}, u32[]{:S(2)}) collective-permute-start(bf16[4,32,768]{2,1,0:T(8,128)(2,1)S(1)} %pad_maximum_fusion), channel_id=1, source_target_pairs={{0,24},{8,16},{16,8},{24,0},{1,25},{9,17},{17,9},{25,1},{2,26},{10... | collective-permute-start | bytes 589832 | tf_op jit(solution)/shard_map/ppermute | solution.py:118
  14.6 1.6 %collective-permute-start.3 = (bf16[48,768]{1,0:T(8,128)(2,1)S(1)}, bf16[48,768]{1,0:T(8,128)(2,1)S(1)}, u32[]{:S(2)}, u32[]{:S(2)}) collective-permute-start(bf16[48,768]{1,0:T(8,128)(2,1)S(1)} %get-tuple-element.33), channel_id=1, source_target_pairs={{0,4},{1,5},{2,6},{3,7},{4,0},{5,1},{6,2},{7,3},{8,12},{9,13},{10,... | collective-permute-start | bytes 221192 | tf_op jit(solution)/shard_map/ppermute | solution.py:118
  16.2 1.0 %collective-permute-start.4 = (bf16[48,768]{1,0:T(8,128)(2,1)S(1)}, bf16[48,768]{1,0:T(8,128)(2,1)S(1)}, u32[]{:S(2)}, u32[]{:S(2)}) collective-permute-start(bf16[48,768]{1,0:T(8,128)(2,1)S(1)} %get-tuple-element.34), channel_id=1, source_target_pairs={{0,6},{1,7},{2,4},{3,5},{4,2},{5,3},{6,0},{7,1},{8,14},{9,15},{10,... | collective-permute-start | bytes 221192 | tf_op jit(solution)/shard_map/ppermute | solution.py:118
  17.2 3.9 %collective-permute-done.3.refs_1_ = bf16[48,768]{1,0:T(8,128)(2,1)S(1)} collective-permute-done((bf16[48,768]{1,0:T(8,128)(2,1)S(1)}, bf16[48,768]{1,0:T(8,128)(2,1)S(1)}, u32[]{:S(2)}, u32[]{:S(2)}) %collective-permute-start.3) | collective-permute-done | bytes 73760 | tf_op jit(solution)/shard_map/ppermute | solution.py:118
  21.2 0.9 %collective-permute-done.11.refs_9_ = bf16[4,32,768]{2,1,0:T(8,128)(2,1)S(1)} collective-permute-done((bf16[4,32,768]{2,1,0:T(8,128)(2,1)S(1)}, bf16[4,32,768]{2,1,0:T(8,128)(2,1)S(1)}, u32[]{:S(2)}, u32[]{:S(2)}) %collective-permute-start.11) | collective-permute-done | bytes 196640 | tf_op jit(solution)/shard_map/ppermute | solution.py:118
  22.0 0.5 %collective-permute-start.13 = (bf16[4,32,768]{2,1,0:T(8,128)(2,1)S(1)}, bf16[4,32,768]{2,1,0:T(8,128)(2,1)S(1)}, u32[]{:S(2)}, u32[]{:S(2)}) collective-permute-start(bf16[4,32,768]{2,1,0:T(8,128)(2,1)S(1)} %collective-permute-done.10.refs_8_), channel_id=1, source_target_pairs={{0,1},{1,0},{2,3},{3,2},{4,5},{5,4},{6,7},{7,6},{8,9},{9,8},{10,11... | collective-permute-start | bytes 589832 | tf_op jit(solution)/shard_map/ppermute | solution.py:122
  22.7 2.8 %collective-permute-done.5.refs_3_ = bf16[48,768]{1,0:T(8,128)(2,1)S(1)} collective-permute-done((bf16[48,768]{1,0:T(8,128)(2,1)S(1)}, bf16[48,768]{1,0:T(8,128)(2,1)S(1)}, u32[]{:S(2)}, u32[]{:S(2)}) %collective-permute-start.5) | collective-permute-done | bytes 73760 | tf_op jit(solution)/shard_map/ppermute | solution.py:118
  25.5 0.5 %collective-permute-start.8 = (bf16[48,768]{1,0:T(8,128)(2,1)S(1)}, bf16[48,768]{1,0:T(8,128)(2,1)S(1)}, u32[]{:S(2)}, u32[]{:S(2)}) collective-permute-start(bf16[48,768]{1,0:T(8,128)(2,1)S(1)} %collective-permute-done.4.refs_2_), channel_id=1, source_target_pairs={{0,1},{1,0},{2,3},{3,2},{4,5},{5,4},{6,7},{7,6},{8,9},{9,8},{10,11... | collective-permute-start | bytes 221192 | tf_op jit(solution)/shard_map/ppermute | solution.py:122
  26.0 0.8 %collective-permute-done.7.refs_5_ = bf16[48,768]{1,0:T(8,128)(2,1)S(1)} collective-permute-done((bf16[48,768]{1,0:T(8,128)(2,1)S(1)}, bf16[48,768]{1,0:T(8,128)(2,1)S(1)}, u32[]{:S(2)}, u32[]{:S(2)}) %collective-permute-start.7) | collective-permute-done | bytes 73760 | tf_op jit(solution)/shard_map/ppermute | solution.py:122
  26.9 1.1 %collective-permute-done.9.refs_7_ = bf16[48,768]{1,0:T(8,128)(2,1)S(1)} collective-permute-done((bf16[48,768]{1,0:T(8,128)(2,1)S(1)}, bf16[48,768]{1,0:T(8,128)(2,1)S(1)}, u32[]{:S(2)}, u32[]{:S(2)}) %collective-permute-start.9) | collective-permute-done | bytes 73760 | tf_op jit(solution)/shard_map/ppermute | solution.py:122
  28.0 0.7 %attend.1 = (bf16[16,768]{1,0:T(8,128)(2,1)S(1)}, bf16[16,768]{1,0:T(8,128)(2,1)S(1)}, bf16[16,768]{1,0:T(8,128)(2,1)S(1)}, bf16[16,768]{1,0:T(8,128)(2,1)S(1)}) custom-call(f32[1,768]{1,0:T(1,128)S(1)} %dynamic_slice.3.gate_ref, bf16[48,768]{1,0:T(8,128)(2,1)S(1)} %get-tuple-element.32.refs_0_, bf16[48,768]{1,0:T(8,128)(2,1)S(1)} %collective-permute-done.3.refs_1_, ...), custom_call_target="tpu_custom_call" | custom-call | tf_op jit(solution)/shard_map/attend/pallas_call | solution.py:237
  28.7 2.1 %collective-permute-start.16 = (bf16[16,768]{1,0:T(8,128)(2,1)S(1)}, bf16[16,768]{1,0:T(8,128)(2,1)S(1)}, u32[]{:S(2)}, u32[]{:S(2)}) collective-permute-start(bf16[16,768]{1,0:T(8,128)(2,1)S(1)} %get-tuple-element.38), channel_id=1, source_target_pairs={{0,6},{1,7},{2,4},{3,5},{4,2},{5,3},{6,0},{7,1},{8,14},{9,15},{10,... | collective-permute-start | bytes 73736 | tf_op jit(solution)/shard_map/ppermute | solution.py:118
  30.8 2.3 %collective-permute-start.18 = (bf16[16,768]{1,0:T(8,128)(2,1)S(1)}, bf16[16,768]{1,0:T(8,128)(2,1)S(1)}, u32[]{:S(2)}, u32[]{:S(2)}) collective-permute-start(bf16[16,768]{1,0:T(8,128)(2,1)S(1)} %get-tuple-element.40), channel_id=1, source_target_pairs={{0,2},{1,3},{2,0},{3,1},{4,6},{5,7},{6,4},{7,5},{8,10},{9,11},{10,... | collective-permute-start | bytes 73736 | tf_op jit(solution)/shard_map/ppermute | solution.py:118
  33.2 1.3 %collective-permute-done.16.refs_1_ = bf16[16,768]{1,0:T(8,128)(2,1)S(1)} collective-permute-done((bf16[16,768]{1,0:T(8,128)(2,1)S(1)}, bf16[16,768]{1,0:T(8,128)(2,1)S(1)}, u32[]{:S(2)}, u32[]{:S(2)}) %collective-permute-start.16) | collective-permute-done | bytes 24608 | tf_op jit(solution)/shard_map/ppermute | solution.py:118
  34.4 1.1 %collective-permute-done.17.refs_2_ = bf16[16,768]{1,0:T(8,128)(2,1)S(1)} collective-permute-done((bf16[16,768]{1,0:T(8,128)(2,1)S(1)}, bf16[16,768]{1,0:T(8,128)(2,1)S(1)}, u32[]{:S(2)}, u32[]{:S(2)}) %collective-permute-start.17) | collective-permute-done | bytes 24608 | tf_op jit(solution)/shard_map/ppermute | solution.py:118
  35.6 0.7 %join.1 = bf16[16,3072]{1,0:T(8,128)(2,1)} custom-call(s32[1]{0:T(128)} %bitcast.level_ref, bf16[16,768]{1,0:T(8,128)(2,1)S(1)} %get-tuple-element.37.refs_0_, bf16[16,768]{1,0:T(8,128)(2,1)S(1)} %collective-permute-done.16.refs_1_, bf16[16,768]{1,0:T(8,128)(2,1)S(1)} %collective-permute-done.17.refs_2_, bf16[16,768]{1,0:T(8,128)(2,1)S(1)} %collective-permute-done.18.refs_3_), custom_call_target="tpu_custom_call" | custom-call | tf_op jit(solution)/shard_map/join/pallas_call | solution.py:245
  (20 shorter events, 0.6 us)
Async XLA Ops:
  1.0 8.2 %collective-permute-start = (bf16[32,768]{1,0:T(8,128)(2,1)S(1)}, bf16[32,768]{1,0:T(8,128)(2,1)S(1)}, u32[]{:S(2)}, u32[]{:S(2)}) collective-permute-start(bf16[32,768]{1,0:T(8,128)(2,1)S(1)} %get-tuple-element.24), channel_id=1, source_target_pairs={{0,4},{1,5},{2,6},{3,7},{4,0},{5,1},{6,2},{7,3},{8,12},{9,13},{10,... | collective-permute-start | bytes 147464 | tf_op jit(solution)/shard_map/ppermute | solution.py:118
  5.1 6.0 %collective-permute-start.1 = (bf16[32,768]{1,0:T(8,128)(2,1)S(1)}, bf16[32,768]{1,0:T(8,128)(2,1)S(1)}, u32[]{:S(2)}, u32[]{:S(2)}) collective-permute-start(bf16[32,768]{1,0:T(8,128)(2,1)S(1)} %get-tuple-element.25), channel_id=1, source_target_pairs={{0,6},{1,7},{2,4},{3,5},{4,2},{5,3},{6,0},{7,1},{8,14},{9,15},{10,... | collective-permute-start | bytes 147464 | tf_op jit(solution)/shard_map/ppermute | solution.py:118
  6.4 4.6 %collective-permute-start.2 = (bf16[32,768]{1,0:T(8,128)(2,1)S(1)}, bf16[32,768]{1,0:T(8,128)(2,1)S(1)}, u32[]{:S(2)}, u32[]{:S(2)}) collective-permute-start(bf16[32,768]{1,0:T(8,128)(2,1)S(1)} %get-tuple-element.26), channel_id=1, source_target_pairs={{0,2},{1,3},{2,0},{3,1},{4,6},{5,7},{6,4},{7,5},{8,10},{9,11},{10,... | collective-permute-start | bytes 147464 | tf_op jit(solution)/shard_map/ppermute | solution.py:118
  11.1 10.1 %collective-permute-start.12 = (bf16[4,32,768]{2,1,0:T(8,128)(2,1)S(1)}, bf16[4,32,768]{2,1,0:T(8,128)(2,1)S(1)}, u32[]{:S(2)}, u32[]{:S(2)}) collective-permute-start(bf16[4,32,768]{2,1,0:T(8,128)(2,1)S(1)} %pad_maximum_fusion), channel_id=1, source_target_pairs={{0,8},{8,0},{16,24},{24,16},{1,9},{9,1},{17,25},{25,17},{2,10},{10... | collective-permute-start | bytes 589832 | tf_op jit(solution)/shard_map/ppermute | solution.py:118
  12.6 9.4 %collective-permute-start.11 = (bf16[4,32,768]{2,1,0:T(8,128)(2,1)S(1)}, bf16[4,32,768]{2,1,0:T(8,128)(2,1)S(1)}, u32[]{:S(2)}, u32[]{:S(2)}) collective-permute-start(bf16[4,32,768]{2,1,0:T(8,128)(2,1)S(1)} %pad_maximum_fusion), channel_id=1, source_target_pairs={{0,16},{8,24},{16,0},{24,8},{1,17},{9,25},{17,1},{25,9},{2,18},{10... | collective-permute-start | bytes 589832 | tf_op jit(solution)/shard_map/ppermute | solution.py:118
  14.2 7.9 %collective-permute-start.10 = (bf16[4,32,768]{2,1,0:T(8,128)(2,1)S(1)}, bf16[4,32,768]{2,1,0:T(8,128)(2,1)S(1)}, u32[]{:S(2)}, u32[]{:S(2)}) collective-permute-start(bf16[4,32,768]{2,1,0:T(8,128)(2,1)S(1)} %pad_maximum_fusion), channel_id=1, source_target_pairs={{0,24},{8,16},{16,8},{24,0},{1,25},{9,17},{17,9},{25,1},{2,26},{10... | collective-permute-start | bytes 589832 | tf_op jit(solution)/shard_map/ppermute | solution.py:118
  14.6 6.5 %collective-permute-start.3 = (bf16[48,768]{1,0:T(8,128)(2,1)S(1)}, bf16[48,768]{1,0:T(8,128)(2,1)S(1)}, u32[]{:S(2)}, u32[]{:S(2)}) collective-permute-start(bf16[48,768]{1,0:T(8,128)(2,1)S(1)} %get-tuple-element.33), channel_id=1, source_target_pairs={{0,4},{1,5},{2,6},{3,7},{4,0},{5,1},{6,2},{7,3},{8,12},{9,13},{10,... | collective-permute-start | bytes 221192 | tf_op jit(solution)/shard_map/ppermute | solution.py:118
  16.2 6.5 %collective-permute-start.4 = (bf16[48,768]{1,0:T(8,128)(2,1)S(1)}, bf16[48,768]{1,0:T(8,128)(2,1)S(1)}, u32[]{:S(2)}, u32[]{:S(2)}) collective-permute-start(bf16[48,768]{1,0:T(8,128)(2,1)S(1)} %get-tuple-element.34), channel_id=1, source_target_pairs={{0,6},{1,7},{2,4},{3,5},{4,2},{5,3},{6,0},{7,1},{8,14},{9,15},{10,... | collective-permute-start | bytes 221192 | tf_op jit(solution)/shard_map/ppermute | solution.py:118
  21.1 4.4 %collective-permute-start.5 = (bf16[48,768]{1,0:T(8,128)(2,1)S(1)}, bf16[48,768]{1,0:T(8,128)(2,1)S(1)}, u32[]{:S(2)}, u32[]{:S(2)}) collective-permute-start(bf16[48,768]{1,0:T(8,128)(2,1)S(1)} %get-tuple-element.35), channel_id=1, source_target_pairs={{0,2},{1,3},{2,0},{3,1},{4,6},{5,7},{6,4},{7,5},{8,10},{9,11},{10,... | collective-permute-start | bytes 221192 | tf_op jit(solution)/shard_map/ppermute | solution.py:118
  21.1 6.9 %collective-permute-start.15 = (bf16[4,32,768]{2,1,0:T(8,128)(2,1)S(1)}, bf16[4,32,768]{2,1,0:T(8,128)(2,1)S(1)}, u32[]{:S(2)}, u32[]{:S(2)}) collective-permute-start(bf16[4,32,768]{2,1,0:T(8,128)(2,1)S(1)} %collective-permute-done.12.refs_10_), channel_id=1, source_target_pairs={{0,1},{1,0},{2,3},{3,2},{4,5},{5,4},{6,7},{7,6},{8,9},{9,8},{10,11... | collective-permute-start | bytes 589832 | tf_op jit(solution)/shard_map/ppermute | solution.py:122
  22.0 6.0 %collective-permute-start.14 = (bf16[4,32,768]{2,1,0:T(8,128)(2,1)S(1)}, bf16[4,32,768]{2,1,0:T(8,128)(2,1)S(1)}, u32[]{:S(2)}, u32[]{:S(2)}) collective-permute-start(bf16[4,32,768]{2,1,0:T(8,128)(2,1)S(1)} %collective-permute-done.11.refs_9_), channel_id=1, source_target_pairs={{0,1},{1,0},{2,3},{3,2},{4,5},{5,4},{6,7},{7,6},{8,9},{9,8},{10,11... | collective-permute-start | bytes 589832 | tf_op jit(solution)/shard_map/ppermute | solution.py:122
  22.0 6.0 %collective-permute-start.13 = (bf16[4,32,768]{2,1,0:T(8,128)(2,1)S(1)}, bf16[4,32,768]{2,1,0:T(8,128)(2,1)S(1)}, u32[]{:S(2)}, u32[]{:S(2)}) collective-permute-start(bf16[4,32,768]{2,1,0:T(8,128)(2,1)S(1)} %collective-permute-done.10.refs_8_), channel_id=1, source_target_pairs={{0,1},{1,0},{2,3},{3,2},{4,5},{5,4},{6,7},{7,6},{8,9},{9,8},{10,11... | collective-permute-start | bytes 589832 | tf_op jit(solution)/shard_map/ppermute | solution.py:122
  22.7 2.8 %collective-permute-start.6 = (bf16[48,768]{1,0:T(8,128)(2,1)S(1)}, bf16[48,768]{1,0:T(8,128)(2,1)S(1)}, u32[]{:S(2)}, u32[]{:S(2)}) collective-permute-start(bf16[48,768]{1,0:T(8,128)(2,1)S(1)} %get-tuple-element.32.refs_0_), channel_id=1, source_target_pairs={{0,1},{1,0},{2,3},{3,2},{4,5},{5,4},{6,7},{7,6},{8,9},{9,8},{10,11... | collective-permute-start | bytes 221192 | tf_op jit(solution)/shard_map/ppermute | solution.py:122
  25.5 1.3 %collective-permute-start.7 = (bf16[48,768]{1,0:T(8,128)(2,1)S(1)}, bf16[48,768]{1,0:T(8,128)(2,1)S(1)}, u32[]{:S(2)}, u32[]{:S(2)}) collective-permute-start(bf16[48,768]{1,0:T(8,128)(2,1)S(1)} %collective-permute-done.3.refs_1_), channel_id=1, source_target_pairs={{0,1},{1,0},{2,3},{3,2},{4,5},{5,4},{6,7},{7,6},{8,9},{9,8},{10,11... | collective-permute-start | bytes 221192 | tf_op jit(solution)/shard_map/ppermute | solution.py:122
  25.5 1.4 %collective-permute-start.8 = (bf16[48,768]{1,0:T(8,128)(2,1)S(1)}, bf16[48,768]{1,0:T(8,128)(2,1)S(1)}, u32[]{:S(2)}, u32[]{:S(2)}) collective-permute-start(bf16[48,768]{1,0:T(8,128)(2,1)S(1)} %collective-permute-done.4.refs_2_), channel_id=1, source_target_pairs={{0,1},{1,0},{2,3},{3,2},{4,5},{5,4},{6,7},{7,6},{8,9},{9,8},{10,11... | collective-permute-start | bytes 221192 | tf_op jit(solution)/shard_map/ppermute | solution.py:122
  26.8 1.3 %collective-permute-start.9 = (bf16[48,768]{1,0:T(8,128)(2,1)S(1)}, bf16[48,768]{1,0:T(8,128)(2,1)S(1)}, u32[]{:S(2)}, u32[]{:S(2)}) collective-permute-start(bf16[48,768]{1,0:T(8,128)(2,1)S(1)} %collective-permute-done.5.refs_3_), channel_id=1, source_target_pairs={{0,1},{1,0},{2,3},{3,2},{4,5},{5,4},{6,7},{7,6},{8,9},{9,8},{10,11... | collective-permute-start | bytes 221192 | tf_op jit(solution)/shard_map/ppermute | solution.py:122
  28.7 5.7 %collective-permute-start.16 = (bf16[16,768]{1,0:T(8,128)(2,1)S(1)}, bf16[16,768]{1,0:T(8,128)(2,1)S(1)}, u32[]{:S(2)}, u32[]{:S(2)}) collective-permute-start(bf16[16,768]{1,0:T(8,128)(2,1)S(1)} %get-tuple-element.38), channel_id=1, source_target_pairs={{0,6},{1,7},{2,4},{3,5},{4,2},{5,3},{6,0},{7,1},{8,14},{9,15},{10,... | collective-permute-start | bytes 73736 | tf_op jit(solution)/shard_map/ppermute | solution.py:118
  30.8 4.7 %collective-permute-start.17 = (bf16[16,768]{1,0:T(8,128)(2,1)S(1)}, bf16[16,768]{1,0:T(8,128)(2,1)S(1)}, u32[]{:S(2)}, u32[]{:S(2)}) collective-permute-start(bf16[16,768]{1,0:T(8,128)(2,1)S(1)} %get-tuple-element.39), channel_id=1, source_target_pairs={{0,4},{1,5},{2,6},{3,7},{4,0},{5,1},{6,2},{7,3},{8,12},{9,13},{10,... | collective-permute-start | bytes 73736 | tf_op jit(solution)/shard_map/ppermute | solution.py:118
  30.8 4.7 %collective-permute-start.18 = (bf16[16,768]{1,0:T(8,128)(2,1)S(1)}, bf16[16,768]{1,0:T(8,128)(2,1)S(1)}, u32[]{:S(2)}, u32[]{:S(2)}) collective-permute-start(bf16[16,768]{1,0:T(8,128)(2,1)S(1)} %get-tuple-element.40), channel_id=1, source_target_pairs={{0,2},{1,3},{2,0},{3,1},{4,6},{5,7},{6,4},{7,5},{8,10},{9,11},{10,... | collective-permute-start | bytes 73736 | tf_op jit(solution)/shard_map/ppermute | solution.py:118
